TPU v7x, 256 devices: a whole 4x4x8 slice. The times are simulated.
256 devices in a mesh: dp: 16 (over x, y), tensor: 16 (over z, core).
Axes of the slice: x: 4, y: 4, z: 8, core: 2. Of those that a mesh axis runs over, the one named last changes fastest.
Arguments:
- hidden: bfloat16 [32768, 1280], P(('dp', 'tensor')), may hold values from -6 to 6
- lengths: int32 [16, 8], P('dp'), may hold values from 1 to 1024, 2048 in all within a row
- request_prompt: int32 [16, 8], P('dp'), may hold values from 0 to 31
- request_adapter: int32 [16, 8], P('dp'), may hold values from 0 to 63
- prompt_page_table: int32 [32, 4], replicated, may hold values from 0 to 63
- prefix_page_cache: bfloat16 [64, 64, 2048], P('dp', None, 'tensor'), may hold values from -6 to 6
- query_key_value_weight: bfloat16 [1280, 3072], P(None, 'tensor'), may hold values from -0.15625 to 0.15625
- adapter_down: bfloat16 [64, 1280, 16], P('dp'), may hold values from -0.15625 to 0.15625
- adapter_up: bfloat16 [64, 16, 3072], P('dp', None, 'tensor'), may hold values from -1.5 to 1.5
- attention_scale: float32 [1024], P('tensor'), may hold values from 0.5 to 1.5
- output_matrix: bfloat16 [1024, 1280], P('tensor'), may hold values from -0.1875 to 0.1875
- attention_rate: float32 [1280], replicated, may hold values from 0.05 to 0.5
- up_matrix: bfloat16 [1280, 5120], P(None, 'tensor'), may hold values from -0.15625 to 0.15625
- gate_matrix: bfloat16 [1280, 5120], P(None, 'tensor'), may hold values from -0.15625 to 0.15625
- up_scaling: float32 [5120], P('tensor'), may hold values from 0.5 to 2
- gate_scaling: float32 [5120], P('tensor'), may hold values from 0.5 to 2
- down_matrix: bfloat16 [5120, 1280], P('tensor'), may hold values from -0.078125 to 0.078125
- feedforward_rate: float32 [1280], replicated, may hold values from 0.05 to 0.5
Outputs:
- hidden_out: bfloat16 [32768, 1280], P(('dp', 'tensor'))
Inputs may be any that keep to these rules, and one draw needn't show every extreme that they name: Each group's lengths sum to 2048.
All inputs are finite; a program needn't handle non-finite values.
Results may differ from a plain program's by a relative error of at most 0.015.
Values may be sent and summed in bfloat16 or wider, within the bound.
A program may use at most 64 MiB of HBM per device.

v0:
```python
import math
import jax
import jax.numpy as jnp
from jax import lax
from jax.sharding import PartitionSpec as P

MODEL_WIDTH = 1280
HEAD_WIDTH = 64
ADAPTER_RANK = 16
GROUP_REQUESTS = 8
PAGE = 64
PREFIX_LEN = 256
adapter_scale = 0.5
epsilon = 1e-06


def renorm(matrix):
    return matrix * lax.rsqrt(jnp.mean(matrix * matrix, axis=-1, keepdims=True) + epsilon)


def to_unit(vectors):
    return vectors * lax.rsqrt(jnp.sum(vectors * vectors, axis=-1, keepdims=True) + epsilon)


def rotate(vectors, position):
    half_size = vectors.shape[-1] // 2
    frequency = jnp.exp(
        jnp.arange(half_size).astype(jnp.float32) * (-2.0 * math.log(10000.0) / vectors.shape[-1])
    )
    angles = position[:, None] * frequency[None, :]
    cosine = jnp.cos(angles)[:, None, :]
    sines = jnp.sin(angles)[:, None, :]
    first_half = vectors[..., :half_size]
    second_half = vectors[..., half_size:]
    return jnp.concatenate(
        [first_half * cosine - second_half * sines, first_half * sines + second_half * cosine],
        axis=-1,
    )


def layout(counts, total_rows):
    row_ends = jnp.cumsum(counts)
    starts = row_ends - counts
    row_ids = jnp.arange(total_rows, dtype=jnp.int32)
    request_number = jnp.sum((row_ids[:, None] >= row_ends[None, :]).astype(jnp.int32), axis=1)
    selected_adapter = (
        request_number[:, None] == jnp.arange(counts.shape[0], dtype=jnp.int32)[None, :]
    )
    offset = row_ids - jnp.sum(jnp.where(selected_adapter, starts[None, :], 0), axis=1)
    return (request_number, offset)


def attend(queries, key_all, value_all, request_number, key_request, key_row):
    rows_total = queries.shape[0]
    block_rows = min(512, rows_total)
    score_scale = math.sqrt(queries.shape[-1])
    row_ids = jnp.arange(rows_total, dtype=jnp.int32)

    def one_block(block_index):
        first_row = block_index * block_rows
        query_block = lax.dynamic_slice_in_dim(queries, first_row, block_rows, 0)
        request_block = lax.dynamic_slice_in_dim(request_number, first_row, block_rows, 0)
        row_block = lax.dynamic_slice_in_dim(row_ids, first_row, block_rows, 0)
        scores = (
            jnp.einsum("qhd,khd->hqk", query_block, key_all, preferred_element_type=jnp.float32)
            * score_scale
        )
        allowed = (request_block[:, None] == key_request[None, :]) & (
            key_row[None, :] <= row_block[:, None]
        )
        exp_scores = jnp.where(allowed[None], jnp.exp(scores), 0.0)
        weights = (exp_scores / jnp.sum(exp_scores, axis=-1, keepdims=True)).astype(jnp.bfloat16)
        mixed_block = jnp.einsum(
            "hqk,khd->qhd", weights, value_all, preferred_element_type=jnp.float32
        )
        return mixed_block.reshape(block_rows, -1).astype(jnp.bfloat16)

    blocks = lax.map(one_block, jnp.arange(rows_total // block_rows, dtype=jnp.int32))
    return blocks.reshape(rows_total, -1)


def hidden_units(row_values, up_matrix, gate_matrix, up_scaling, gate_scaling):
    up_part = jnp.dot(row_values, up_matrix, preferred_element_type=jnp.float32) * up_scaling
    gate_part = jnp.dot(row_values, gate_matrix, preferred_element_type=jnp.float32) * gate_scaling
    return (up_part * jax.nn.silu(gate_part)).astype(jnp.bfloat16)


def local(
    hidden,
    lengths,
    request_prompt,
    request_adapter,
    prompt_page_table,
    prefix_page_cache,
    query_key_value_weight,
    adapter_down,
    adapter_up,
    attention_scale,
    output_matrix,
    attention_rate,
    up_matrix,
    gate_matrix,
    up_scaling,
    gate_scaling,
    down_matrix,
    feedforward_rate,
):
    tok_rows = hidden.shape[0]
    group_rows = tok_rows * lax.axis_size("tensor")
    heads_here = query_key_value_weight.shape[1] // (3 * HEAD_WIDTH)
    gain_qk = attention_scale.reshape(heads_here, HEAD_WIDTH)
    request_number, offset = layout(lengths[0], group_rows)
    position = offset.astype(jnp.float32) + PREFIX_LEN
    local_cache = prefix_page_cache.reshape(
        prefix_page_cache.shape[0], PAGE, heads_here, 2, HEAD_WIDTH
    )
    local_keys = (to_unit(local_cache[:, :, :, 0, :].astype(jnp.float32)) * gain_qk).astype(
        jnp.bfloat16
    )
    prepared = jnp.stack([local_keys, local_cache[:, :, :, 1, :]], axis=3).reshape(
        prefix_page_cache.shape
    )
    all_pages = lax.all_gather(prepared, "dp", axis=0, tiled=True)
    down_all, up_all = (
        lax.all_gather(adapter_down, "dp", axis=0, tiled=True),
        lax.all_gather(adapter_up, "dp", axis=0, tiled=True),
    )
    every_row = lax.all_gather(hidden, "tensor", axis=0, tiled=True)
    adapter_count = down_all.shape[0]
    onehot = (
        request_adapter[0][:, None] == jnp.arange(adapter_count, dtype=jnp.int32)[None, :]
    ).astype(jnp.bfloat16)
    selected_down = jnp.dot(
        onehot, down_all.reshape(adapter_count, -1), preferred_element_type=jnp.float32
    ).astype(jnp.bfloat16)
    selected_down = jnp.transpose(
        selected_down.reshape(GROUP_REQUESTS, MODEL_WIDTH, ADAPTER_RANK), (1, 0, 2)
    ).reshape(MODEL_WIDTH, GROUP_REQUESTS * ADAPTER_RANK)
    selected_up = jnp.dot(
        onehot, up_all.reshape(adapter_count, -1), preferred_element_type=jnp.float32
    ).astype(jnp.bfloat16)
    selected_up = selected_up.reshape(GROUP_REQUESTS * ADAPTER_RANK, heads_here * 3 * HEAD_WIDTH)
    request_of_slot = jnp.arange(GROUP_REQUESTS * ADAPTER_RANK, dtype=jnp.int32) // ADAPTER_RANK
    plain_projection = jnp.dot(
        every_row, query_key_value_weight, preferred_element_type=jnp.float32
    )
    adapter_middle = jnp.dot(every_row, selected_down, preferred_element_type=jnp.float32)
    adapter_middle = jnp.where(
        request_number[:, None] == request_of_slot[None, :], adapter_middle, 0.0
    ).astype(jnp.bfloat16)
    query_key_value = (
        plain_projection
        + adapter_scale * jnp.dot(adapter_middle, selected_up, preferred_element_type=jnp.float32)
    ).reshape(group_rows, heads_here, 3, HEAD_WIDTH)
    queries = (to_unit(rotate(query_key_value[:, :, 0, :], position)) * gain_qk).astype(
        jnp.bfloat16
    )
    key_own = (to_unit(rotate(query_key_value[:, :, 1, :], position)) * gain_qk).astype(
        jnp.bfloat16
    )
    value_own = query_key_value[:, :, 2, :].astype(jnp.bfloat16)
    page_list = prompt_page_table[request_prompt[0]].reshape(-1)
    picked = jnp.take(all_pages, page_list, axis=0).reshape(
        GROUP_REQUESTS * PREFIX_LEN, heads_here, 2, HEAD_WIDTH
    )
    key_all = jnp.concatenate([picked[:, :, 0, :], key_own], axis=0)
    value_all = jnp.concatenate([picked[:, :, 1, :], value_own], axis=0)
    key_request = jnp.concatenate(
        [jnp.arange(GROUP_REQUESTS * PREFIX_LEN, dtype=jnp.int32) // PREFIX_LEN, request_number],
        axis=0,
    )
    key_row = jnp.concatenate(
        [
            jnp.full((GROUP_REQUESTS * PREFIX_LEN,), -1, jnp.int32),
            jnp.arange(group_rows, dtype=jnp.int32),
        ],
        axis=0,
    )
    attn = attend(queries, key_all, value_all, request_number, key_request, key_row)
    attn_sum = lax.psum_scatter(
        jnp.dot(attn, output_matrix, preferred_element_type=jnp.float32).astype(jnp.bfloat16),
        "tensor",
        scatter_dimension=0,
        tiled=True,
    ).astype(jnp.float32)
    base_rows = hidden.astype(jnp.float32)
    mixed = renorm(base_rows + attention_rate * (renorm(attn_sum) - base_rows)).astype(jnp.bfloat16)
    unit_values = hidden_units(
        lax.all_gather(mixed, "tensor", axis=0, tiled=True),
        up_matrix,
        gate_matrix,
        up_scaling,
        gate_scaling,
    )
    mlp_sum = lax.psum_scatter(
        jnp.dot(unit_values, down_matrix, preferred_element_type=jnp.float32).astype(jnp.bfloat16),
        "tensor",
        scatter_dimension=0,
        tiled=True,
    ).astype(jnp.float32)
    mixed_rows = mixed.astype(jnp.float32)
    return renorm(mixed_rows + feedforward_rate * (renorm(mlp_sum) - mixed_rows)).astype(
        jnp.bfloat16
    )


def solution(mesh):
    placed = (
        P(("dp", "tensor"), None),
        P("dp", None),
        P("dp", None),
        P("dp", None),
        P(),
        P("dp", None, "tensor"),
        P(None, "tensor"),
        P("dp", None, None),
        P("dp", None, "tensor"),
        P("tensor"),
        P("tensor", None),
        P(),
        P(None, "tensor"),
        P(None, "tensor"),
        P("tensor"),
        P("tensor"),
        P("tensor", None),
        P(),
    )
    return jax.shard_map(
        local, mesh=mesh, in_specs=placed, out_specs=P(("dp", "tensor"), None), check_vma=False
    )
```

profile of v0, /device:TPU:8, one launch (start us, length us, event | category | flops | bytes accessed | tf_op | source)
XLA Modules:
  0.0 397.9 jit_solution(10989033186772423542)
XLA Ops:
  6.5 1.0 reshape.596
  7.6 0.6 multiply_reduce_fusion.4
  8.3 1.0 multiply_convert_fusion.4
  9.7 0.7 reshape.597
  10.5 0.7 all-gather.7.cloned.1.call-update
  11.3 0.7 all-gather.5.cloned.1.call-update
  12.0 0.8 copy.41
  12.8 0.7 fusion.40
  14.1 0.8 reduce-window.4
  15.0 24.1 %all_gather.17 = bf16[64,16,192]{2,1,0:T(8,128)(2,1)S(1)} all-gather(bf16[4,16,192]{2,1,0:T(8,128)(2,1)} %param.28), channel_id=1, replica_groups=mesh['dp'=16,'tensor'=16] {'dp'}, dimensions={0}, use_global_device_ids=true | all-gather | bytes 417792 | tf_op jit(solution)/shard_map/all_gather | solution.py:126
  39.6 0.9 convolution_convert_fusion.3
  41.0 0.7 fusion.42
  41.7 19.0 %all-gather.9.cloned.1.call-done = bf16[64,64,128]{2,1,0:T(8,128)(2,1)} async-done(((bf16[4,64,128]{2,1,0:T(8,128)(2,1)}), bf16[64,64,128]{2,1,0:T(8,128)(2,1)}) %all-gather.9.cloned.1.call-update) | async-done | bytes 1048592 | tf_op jit(solution)/shard_map/all_gather | solution.py:123
  60.8 1.9 gather_fusion.1
  63.1 0.9 copy.44
  64.1 0.9 slice_bitcast_fusion.2
  64.9 49.1 %all-gather.7.cloned.1.call-done = bf16[64,1280,16]{1,2,0:T(8,128)(2,1)} async-done(((bf16[4,1280,16]{1,2,0:T(8,128)(2,1)}), bf16[64,1280,16]{1,2,0:T(8,128)(2,1)}) %all-gather.7.cloned.1.call-update) | async-done | bytes 2621456 | tf_op jit(solution)/shard_map/all_gather | solution.py:125
  114.0 9.7 %copy.39 = bf16[64,1280,16]{0,2,1:T(8,128)(2,1)} copy(bf16[64,1280,16]{1,2,0:T(8,128)(2,1)} %all-gather.7.cloned.1.call-done) | data formatting | bytes 5242880 | tf_op jit(solution)/shard_map/all_gather | solution.py:125
  123.7 4.7 %convolution_convert_fusion = bf16[8,20480]{1,0:T(8,128)(2,1)} fusion(bf16[64,20480]{0,1:T(8,128)(2,1)} %bitcast.89, s32[8]{0:T(128)S(1)} %bitcast.97), kind=kOutput, calls=%fused_computation.13 | convolution fusion | flops 21135872 | bytes 2949152 | tf_op jit(solution)/shard_map/dot_general | solution.py:133
  128.4 2.9 reshape.589
  131.3 1.6 copy.40
  132.9 26.0 %all-gather.5.cloned.1.call-done = bf16[2048,1280]{1,0:T(8,128)(2,1)} async-done(((bf16[128,1280]{1,0:T(8,128)(2,1)}), bf16[2048,1280]{1,0:T(8,128)(2,1)}) %all-gather.5.cloned.1.call-update) | async-done | bytes 5242896 | tf_op jit(solution)/shard_map/all_gather | solution.py:128
  158.9 5.6 %fusion.46 = f32[2048,192]{0,1:T(8,128)} fusion(bf16[2048,1280]{1,0:T(8,128)(2,1)} %all-gather.5.cloned.1.call-done, bf16[1280,192]{0,1:T(8,128)(2,1)} %param.26), kind=kOutput, calls=%fused_computation.120 | convolution fusion | flops 1006632960 | bytes 7307264 | tf_op jit(solution)/shard_map/dot_general | solution.py:144
  164.6 5.0 %fusion.11 = f32[2048,192]{0,1:T(8,128)S(1)} fusion(f32[2048,192]{0,1:T(8,128)} %fusion.46, bf16[128,192]{1,0:T(8,128)(2,1)S(1)} %reshape.592, bf16[1280,128]{0,1:T(8,128)(2,1)S(1)} %bitcast.94, bf16[2048,1280]{1,0:T(8,128)(2,1)} %all-gather.5.cloned.1.call-done, s32[2048]{0:T(1024)S(1)} %convert_reduce_fusion, s32[128]{0:T(128)S(1)} %and_select_fusion), kind=kOutput, calls=%fused_computation.22 | convolution fusion | flops 773324800 | bytes 8774144 | tf_op jit(solution)/shard_map/dot_general | solution.py:153
  169.7 1.2 fusion.32
  171.5 22.6 %while.11 = (s32[]{:T(128)}, bf16[4,512,64]{1,2,0:T(8,128)(2,1)S(1)}, s32[4]{0:T(128)S(1)}, s32[2048]{0:T(1024)S(1)}, s32[4096]{0:T(1024)S(1)}, /*index=5*/s32[2...) while((s32[]{:T(128)}, ...), condition=%wide.region_8.9_spmd, body=%wide.region_6.8_spmd.sunk | while | flops 553680384 | bytes 18006224 | solution.py:78
  171.5 0.6 dynamic_slice.32
  172.9 2.7 fusion.65
  175.5 1.5 fusion.66
  177.1 0.6 dynamic_slice.32
  178.5 2.7 fusion.65
  181.1 1.5 fusion.66
  184.1 2.7 fusion.65
  186.7 1.5 fusion.66
  189.7 2.7 fusion.65
  192.3 1.5 fusion.66
  194.1 3.9 convolution_convert_fusion.2
  198.1 63.4 %reduce-scatter.3.cloned.1.call-done = bf16[128,1280]{1,0:T(8,128)(2,1)} async-done(((bf16[2048,1280]{1,0:T(8,128)(2,1)}), bf16[128,1280]{1,0:T(8,128)(2,1)}) %reduce-scatter.3.cloned.1.call-update) | async-done | bytes 327696 | tf_op jit(solution)/shard_map/reduce_scatter | solution.py:180
  261.5 1.1 fusion.16
  262.6 1.3 multiply_reduce_fusion.1
  264.0 2.1 multiply_convert_fusion.1
  266.1 42.1 %all-gather.11.cloned.1.call-done = bf16[2048,1280]{1,0:T(8,128)(2,1)} async-done(((bf16[128,1280]{1,0:T(8,128)(2,1)}), bf16[2048,1280]{1,0:T(8,128)(2,1)}) %all-gather.11.cloned.1.call-update) | async-done | bytes 5242896 | tf_op jit(solution)/shard_map/all_gather | solution.py:189
  308.2 5.9 %convolution_multiply_fusion = f32[2048,320]{0,1:T(8,128)} fusion(bf16[2048,1280]{1,0:T(8,128)(2,1)} %all-gather.11.cloned.1.call-done, bf16[1280,320]{0,1:T(8,128)(2,1)S(1)} %copy-done.12, f32[320]{0:T(512)S(1)} %copy-done.14), kind=kOutput, calls=%fused_computation.17 | convolution fusion | flops 1678376960 | bytes 8684800 | tf_op jit(solution)/shard_map/dot_general | solution.py:84
  314.1 8.7 %convolution_convert_fusion.1 = bf16[2048,1280]{1,0:T(8,128)(2,1)} fusion(bf16[320,1280]{1,0:T(8,128)(2,1)S(1)} %copy-done, bf16[2048,1280]{1,0:T(8,128)(2,1)} %all-gather.11.cloned.1.call-done, bf16[1280,320]{0,1:T(8,128)(2,1)S(1)} %copy-done.13, f32[2048,320]{0,1:T(8,128)} %convolution_multiply_fusion, f32[320]{0:T(512)S(1)} %copy-done.15), kind=kOutput, calls=%fused_computation.14 | convolution fusion | flops 3362652160 | bytes 14746880 | tf_op jit(solution)/shard_map/dot_general | solution.py:196
  322.9 63.6 %reduce-scatter.5.cloned.1.call-done = bf16[128,1280]{1,0:T(8,128)(2,1)} async-done(((bf16[2048,1280]{1,0:T(8,128)(2,1)}), bf16[128,1280]{1,0:T(8,128)(2,1)}) %reduce-scatter.5.cloned.1.call-update) | async-done | bytes 327696 | tf_op jit(solution)/shard_map/reduce_scatter | solution.py:195
  386.5 1.1 fusion.18
  387.6 1.3 multiply_reduce_fusion
  389.0 2.1 multiply_convert_fusion
  (93 shorter events, 5.4 us)
Async XLA Ops:
  6.5 307.6 %copy-start = (bf16[320,1280]{1,0:T(8,128)(2,1)S(1)}, bf16[320,1280]{1,0:T(8,128)(2,1)}, u32[]{:S(2)}) copy-start(bf16[320,1280]{1,0:T(8,128)(2,1)} %param.36) | copy-start | bytes 2457604
  6.5 54.2 %all-gather.9.cloned.1.call-start = ((), (), s32[]{:S(2)}) async-start(), calls=%async_computation.4 | async-start | bytes 1114112 | tf_op jit(solution)/shard_map/all_gather | solution.py:123
  10.5 103.5 %all-gather.7.cloned.1.call-start = ((), (), s32[]{:S(2)}) async-start(), calls=%async_computation.3 | async-start | bytes 2785280 | tf_op jit(solution)/shard_map/all_gather | solution.py:125
  11.2 147.7 %all-gather.5.cloned.1.call-start = ((), (), s32[]{:S(2)}) async-start(), calls=%async_computation.2 | async-start | bytes 5570560 | tf_op jit(solution)/shard_map/all_gather | solution.py:128
  12.0 249.5 %reduce-scatter.3.cloned.1.call-start = ((), (), s32[]{:S(2)}) async-start(), calls=%async_computation.5 | async-start | bytes 5570560 | tf_op jit(solution)/shard_map/reduce_scatter | solution.py:180
  64.0 59.7 %copy-start.11 = (s32[1,8]{1,0:T(1,128)S(1)}, s32[1,8]{1,0:T(1,128)}, u32[]{:S(2)}) copy-start(s32[1,8]{1,0:T(1,128)} %param.23) | copy-start | bytes 100
  132.9 31.6 %copy-start.3 = (bf16[1280,8,16]{0,2,1:T(8,128)(2,1)S(1)}, bf16[1280,8,16]{0,2,1:T(8,128)(2,1)}, u32[]{:S(2)}) copy-start(bf16[1280,8,16]{0,2,1:T(8,128)(2,1)} %copy.40) | copy-start | bytes 983044
  164.6 6.5 %copy-start.10 = (f32[64]{0:T(128)S(1)}, f32[64]{0:T(128)}, u32[]{:S(2)}) copy-start(f32[64]{0:T(128)} %param.29) | copy-start | bytes 772
  169.6 1.7 copy-start.5
  169.6 1.8 copy-start.4
  169.6 1.8 copy-start.6
  169.6 1.8 copy-start.16
  171.4 22.7 %copy-start.7 = (bf16[64,1280]{1,0:T(8,128)(2,1)S(1)}, bf16[64,1280]{1,0:T(8,128)(2,1)}, u32[]{:S(2)}) copy-start(bf16[64,1280]{1,0:T(8,128)(2,1)} %param.30) | copy-start | bytes 491524
  198.0 64.6 %copy-start.2 = (bf16[128,1280]{1,0:T(8,128)(2,1)S(1)}, bf16[128,1280]{1,0:T(8,128)(2,1)}, u32[]{:S(2)}) copy-start(bf16[128,1280]{1,0:T(8,128)(2,1)} %param.20) | copy-start | bytes 983044
  198.0 64.6 %copy-start.8 = (f32[1280]{0:T(1024)S(1)}, f32[1280]{0:T(1024)}, u32[]{:S(2)}) copy-start(f32[1280]{0:T(1024)} %param.31) | copy-start | bytes 15364
  198.0 110.2 %copy-start.12 = (bf16[1280,320]{0,1:T(8,128)(2,1)S(1)}, bf16[1280,320]{0,1:T(8,128)(2,1)}, u32[]{:S(2)}) copy-start(bf16[1280,320]{0,1:T(8,128)(2,1)} %param.33) | copy-start | bytes 2457604
  198.0 110.2 %copy-start.14 = (f32[320]{0:T(512)S(1)}, f32[320]{0:T(512)}, u32[]{:S(2)}) copy-start(f32[320]{0:T(512)} %param.35) | copy-start | bytes 3844
  198.0 110.2 %all-gather.11.cloned.1.call-start = ((), (), s32[]{:S(2)}) async-start(), calls=%async_computation.6 | async-start | bytes 5570560 | tf_op jit(solution)/shard_map/all_gather | solution.py:189
  266.1 48.1 %copy-start.13 = (bf16[1280,320]{0,1:T(8,128)(2,1)S(1)}, bf16[1280,320]{0,1:T(8,128)(2,1)}, u32[]{:S(2)}) copy-start(bf16[1280,320]{0,1:T(8,128)(2,1)} %param.32) | copy-start | bytes 2457604
  266.1 48.0 %copy-start.15 = (f32[320]{0:T(512)S(1)}, f32[320]{0:T(512)}, u32[]{:S(2)}) copy-start(f32[320]{0:T(512)} %param.34) | copy-start | bytes 3844
  266.1 120.4 %reduce-scatter.5.cloned.1.call-start = ((), (), s32[]{:S(2)}) async-start(), calls=%async_computation.7 | async-start | bytes 5570560 | tf_op jit(solution)/shard_map/reduce_scatter | solution.py:195
  322.8 64.8 %copy-start.1 = (bf16[128,1280]{1,0:T(8,128)(2,1)S(1)}, bf16[128,1280]{1,0:T(8,128)(2,1)}, u32[]{:S(2)}) copy-start(bf16[128,1280]{1,0:T(8,128)(2,1)} %multiply_convert_fusion.1) | copy-start | bytes 983044
  322.8 64.8 %copy-start.9 = (f32[1280]{0:T(1024)S(1)}, f32[1280]{0:T(1024)}, u32[]{:S(2)}) copy-start(f32[1280]{0:T(1024)} %param.37) | copy-start | bytes 15364
Sparse Core Ops, SparseCore 0:
  10.6 50.1 all-gather.8
  63.3 50.6 all-gather.6
  115.8 43.0 all-gather.4
  198.1 63.3 reduce-scatter.2
  266.2 41.9 all-gather.10
  323.0 63.4 reduce-scatter.4
where the time goes:
time: 399 us; the launch traced here: 398 us
  waiting for transfers between devices  265 us (66%)
  matrix products  51.4 us (13%)
  local copies, waits for them, and re-layouts  25.6 us (6%)
  blocking collectives  24.1 us (6%)
  other arithmetic  15.1 us (4%)
  between operations  13.9 us (3%)
    reduce_scatter x1, waiting for transfers between devices, local(): lax.psum_scatter(jnp.dot(unit_values, down_matrix, preferred_element_type...  63.6 us
    reduce_scatter x1, waiting for transfers between devices, local(): lax.psum_scatter(jnp.dot(attn, output_matrix, preferred_element_type=jnp....  63.4 us
    all_gather x1, waiting for transfers between devices, local(): lax.all_gather(adapter_down, 'dp', axis=0, tiled=True)  49.1 us
    all_gather x1, waiting for transfers between devices, local(): lax.all_gather(mixed, 'tensor', axis=0, tiled=True)  42.1 us
    all_gather x1, waiting for transfers between devices, local(): every_row = lax.all_gather(hidden, 'tensor', axis=0, tiled=True)  26 us
    all_gather x1, blocking collectives, local(): lax.all_gather(adapter_up, 'dp', axis=0, tiled=True)  24.1 us
    all_gather x1, waiting for transfers between devices, local(): all_pages = lax.all_gather(prepared, 'dp', axis=0, tiled=True)  19 us
    dot_general x4, matrix products, one_block(): jnp.einsum('qhd,khd->hqk', query_block, key_all, preferred_element_type=j...  10.7 us
  transfers between devices with their start and end apart: 6, of which 6 were waited for; matrix products, arithmetic and copies ran while one was open for 7% of the time, Pallas kernels for 0%

commit v1 on v0

--- a/solution.py
+++ b/solution.py
@@ -1,3 +1,4 @@
+import functools
 import math
 import jax
 import jax.numpy as jnp
@@ -12,6 +13,38 @@
 PREFIX_LEN = 256
 adapter_scale = 0.5
 epsilon = 1e-06
+
+
+def fill_shelves_up(s0, shard_axis):
+    v_now, e_next, current_value = (
+        jax.lax.axis_size(shard_axis),
+        jax.lax.axis_index(shard_axis),
+        s0.shape[0],
+    )
+    crops = []
+    for t in range(v_now):
+        crops.append((t, (t + 1) % v_now))
+    store = []
+    for t in range(v_now):
+        store.append((t, (t - 1) % v_now))
+    long_array = jnp.zeros((*s0.shape[:0], v_now * current_value, *s0.shape[1:]), s0.dtype)
+    long_array = lax.dynamic_update_slice_in_dim(long_array, s0, e_next * current_value, axis=0)
+    parts_out = local_next = s0
+    wide_out = v_now // 2
+    for j0 in range(1, wide_out + 1):
+        parts_out = jax.lax.ppermute(parts_out, axis_name=shard_axis, perm=crops)
+        long_array = lax.dynamic_update_slice_in_dim(
+            long_array, parts_out, (e_next - j0) % v_now * current_value, axis=0
+        )
+        if j0 < v_now - wide_out:
+            local_next = jax.lax.ppermute(local_next, axis_name=shard_axis, perm=store)
+            long_array = lax.dynamic_update_slice_in_dim(
+                long_array, local_next, (e_next + j0) % v_now * current_value, axis=0
+            )
+    return long_array
+
+
+cycles_part = functools.partial(fill_shelves_up, shard_axis="tensor")
 
 
 def renorm(matrix):
@@ -125,7 +158,7 @@
         lax.all_gather(adapter_down, "dp", axis=0, tiled=True),
         lax.all_gather(adapter_up, "dp", axis=0, tiled=True),
     )
-    every_row = lax.all_gather(hidden, "tensor", axis=0, tiled=True)
+    every_row = cycles_part(hidden)
     adapter_count = down_all.shape[0]
     onehot = (
         request_adapter[0][:, None] == jnp.arange(adapter_count, dtype=jnp.int32)[None, :]

time: 399 us -> 371 us (0.930)
  waiting for transfers between devices: 265 us -> 200 us
  starting transfers between devices: 0.2 us -> 23.8 us
  local copies, waits for them, and re-layouts: 25.6 us -> 40.5 us
    all_gather x1, waiting for transfers between devices: 49.1 us -> 8.76 us  [local(): lax.all_gather(adapter_down, 'dp', axis=0, tiled=True)]
    all_gather x1 -> x0, waiting for transfers between devices: 26 us -> none  [local(): every_row = lax.all_gather(hidden, 'tensor', axis=0, tiled=True)]
    ppermute x0 -> x15, starting transfers between devices: none -> 23.6 us  [the longest x7 23.6 us: fill_shelves_up(): local_next = jax.lax.ppermute(local_next, axis_name=shard_axis, perm=store)]
    ppermute x0 -> x15, waiting for transfers between devices: none -> 21.3 us  [the longest x8 21.1 us: fill_shelves_up(): parts_out = jax.lax.ppermute(parts_out, axis_name=shard_axis, perm=crops)]
    all_gather x1, waiting for transfers between devices: 19 us -> 0.01 us  [local(): all_pages = lax.all_gather(prepared, 'dp', axis=0, tiled=True)]
    dynamic_update_slice x0 -> x16, local copies, waits for them, and re-layouts: none -> 13 us  [the longest x7 6.2 us: fill_shelves_up(): lax.dynamic_update_slice_in_dim(long_array, local_next, (e_next + j0) % v...]
  transfers between devices with their start and end apart: 6 -> 20, of which waited for: 6 -> 11; matrix products, arithmetic and copies ran while one was open for 7% -> 7% of each run, Pallas kernels for 0% -> 0%
where the time goes in v1:
time: 371 us; the launch traced here: 370 us
  waiting for transfers between devices  200 us (54%)
  matrix products  49.3 us (13%)
  local copies, waits for them, and re-layouts  40.5 us (11%)
  blocking collectives  24 us (6%)
  starting transfers between devices  23.8 us (6%)
  other arithmetic  15.9 us (4%)
  between operations  13.9 us (4%)
    reduce_scatter x1, waiting for transfers between devices, local(): lax.psum_scatter(jnp.dot(attn, output_matrix, preferred_element_type=jnp....  64.7 us
    reduce_scatter x1, waiting for transfers between devices, local(): lax.psum_scatter(jnp.dot(unit_values, down_matrix, preferred_element_type...  63.5 us
    all_gather x1, waiting for transfers between devices, local(): lax.all_gather(mixed, 'tensor', axis=0, tiled=True)  41.9 us
    all_gather x1, blocking collectives, local(): lax.all_gather(adapter_up, 'dp', axis=0, tiled=True)  24 us
    ppermute x7, starting transfers between devices, fill_shelves_up(): local_next = jax.lax.ppermute(local_next, axis_name=shard_axis, perm=store)  23.6 us
    ppermute x8, waiting for transfers between devices, fill_shelves_up(): parts_out = jax.lax.ppermute(parts_out, axis_name=shard_axis, perm=crops)  21.1 us
    dot_general x4, matrix products, one_block(): jnp.einsum('qhd,khd->hqk', query_block, key_all, preferred_element_type=j...  10.7 us
    all_gather x1, local copies, waits for them, and re-layouts, local(): lax.all_gather(adapter_down, 'dp', axis=0, tiled=True)  9.71 us
  transfers between devices with their start and end apart: 20, of which 11 were waited for; matrix products, arithmetic and copies ran while one was open for 7% of the time, Pallas kernels for 0%

profile of v1, /device:TPU:8, one launch (start us, length us, event | category | flops | bytes accessed | tf_op | source)
XLA Modules:
  0.0 370.5 jit_solution(18183507783349604898)
XLA Ops:
  6.5 1.0 reshape.596
  8.4 1.0 multiply_convert_fusion.4
  10.6 5.3 %collective-permute-start.1 = (bf16[128,1280]{1,0:T(8,128)(2,1)}, bf16[128,1280]{1,0:T(8,128)(2,1)S(1)}, u32[]{:S(2)}, u32[]{:S(2)}) collective-permute-start(bf16[128,1280]{1,0:T(8,128)(2,1)} %param.20), channel_id=1, source_target_pairs={{0,15},{1,0},{2,1},{3,2},{4,3},{5,4},{6,5},{7,6},{8,7},{9,8},{10,9... | collective-permute-start | bytes 983048 | tf_op jit(solution)/shard_map/ppermute | solution.py:40
  19.3 24.0 %all_gather.13 = bf16[64,16,192]{2,1,0:T(8,128)(2,1)S(1)} all-gather(bf16[4,16,192]{2,1,0:T(8,128)(2,1)} %param.28), channel_id=1, replica_groups=mesh['dp'=16,'tensor'=16] {'dp'}, dimensions={0}, use_global_device_ids=true | all-gather | bytes 417792 | tf_op jit(solution)/shard_map/all_gather | solution.py:159
  45.9 2.6 broadcast_in_dim.41
  49.3 3.0 collective-permute-start.3
  53.7 3.2 collective-permute-done.2
  57.0 3.0 collective-permute-start.5
  61.4 3.2 collective-permute-done.4
  64.7 3.0 collective-permute-start.7
  69.2 3.2 collective-permute-done.6
  72.4 3.0 collective-permute-start.9
  76.8 3.3 collective-permute-done.8
  80.1 3.4 collective-permute-start.11
  85.0 2.8 collective-permute-done.10
  88.1 3.1 collective-permute-start.13
  92.7 1.9 gather_fusion.1
  97.5 1.7 constant_dynamic-update-slice_fusion.1
  99.2 5.2 %collective-permute-done.14 = bf16[128,1280]{1,0:T(8,128)(2,1)S(1)} collective-permute-done((bf16[128,1280]{1,0:T(8,128)(2,1)S(1)}, bf16[128,1280]{1,0:T(8,128)(2,1)S(1)}, u32[]{:S(2)}, u32[]{:S(2)}) %collective-permute-start.14) | collective-permute-done | bytes 327712 | tf_op jit(solution)/shard_map/ppermute | solution.py:35
  105.2 8.8 %all-gather.4.cloned.1.call-done = bf16[64,1280,16]{1,2,0:T(8,128)(2,1)} async-done(((bf16[4,1280,16]{1,2,0:T(8,128)(2,1)}), bf16[64,1280,16]{1,2,0:T(8,128)(2,1)}) %all-gather.4.cloned.1.call-update) | async-done | bytes 2621456 | tf_op jit(solution)/shard_map/all_gather | solution.py:158
  114.0 9.7 %copy.39 = bf16[64,1280,16]{0,2,1:T(8,128)(2,1)} copy(bf16[64,1280,16]{1,2,0:T(8,128)(2,1)} %all-gather.4.cloned.1.call-done) | data formatting | bytes 5242880 | tf_op jit(solution)/shard_map/all_gather | solution.py:158
  123.7 4.7 %convolution_convert_fusion = bf16[8,20480]{1,0:T(8,128)(2,1)} fusion(bf16[64,20480]{0,1:T(8,128)(2,1)} %bitcast.81, s32[8]{0:T(128)S(1)} %bitcast.89), kind=kOutput, calls=%fused_computation.13 | convolution fusion | flops 21135872 | bytes 2949152 | tf_op jit(solution)/shard_map/dot_general | solution.py:166
  128.4 2.9 reshape.589
  131.3 1.6 copy.40
  133.0 4.1 %convolution_multiply_fusion.2 = f32[2048,192]{0,1:T(8,128)S(1)} fusion(bf16[128,192]{1,0:T(8,128)(2,1)S(1)} %reshape.592, bf16[2048,1280]{1,0:T(8,128)(2,1)} %constant_dynamic-update-slice_fusion, bf16[1280,128]{0,1:T(8,128)(2,1)} %bitcast.86, s32[128]{0:T(128)S(1)} %and_select_fusion, s32[2048]{0:T(1024)S(1)} %convert_reduce_fusion), kind=kOutput, calls=%fused_computation.21 | convolution fusion | flops 772931584 | bytes 7201280 | tf_op jit(solution)/shard_map/dot_general | solution.py:186
  137.1 4.4 %convolution_add_fusion = f32[2048,192]{0,1:T(8,128)S(1)} fusion(f32[2048,192]{0,1:T(8,128)S(1)} %convolution_multiply_fusion.2, bf16[2048,1280]{1,0:T(8,128)(2,1)} %constant_dynamic-update-slice_fusion, bf16[1280,192]{0,1:T(8,128)(2,1)S(1)} %copy-done.5), kind=kOutput, calls=%fused_computation.22 | convolution fusion | flops 1007026176 | bytes 8880128 | tf_op jit(solution)/shard_map/dot_general | solution.py:177
  141.7 1.2 fusion.30
  143.4 22.6 %while.11 = (s32[]{:T(128)}, bf16[4,512,64]{1,2,0:T(8,128)(2,1)S(1)}, s32[4]{0:T(128)S(1)}, s32[2048]{0:T(1024)S(1)}, s32[4096]{0:T(1024)S(1)}, /*index=5*/s32[2...) while((s32[]{:T(128)}, ...), condition=%wide.region_8.9_spmd, body=%wide.region_6.8_spmd.sunk | while | flops 553680384 | bytes 18006224 | solution.py:111
  144.8 2.7 fusion.62
  147.5 1.5 fusion.63
  150.4 2.7 fusion.62
  153.1 1.5 fusion.63
  156.0 2.7 fusion.62
  158.7 1.5 fusion.63
  161.6 2.7 fusion.62
  164.3 1.5 fusion.63
  166.1 3.9 %convolution_convert_fusion.2 = bf16[2048,1280]{1,0:T(8,128)(2,1)} fusion(bf16[2048,64]{0,1:T(8,128)(2,1)S(1)} %bitcast.85, bf16[64,1280]{1,0:T(8,128)(2,1)S(1)} %copy-done.7), kind=kOutput, calls=%fused_computation.15 | convolution fusion | flops 338165760 | bytes 5668864 | tf_op jit(solution)/shard_map/dot_general | solution.py:214
  170.0 64.7 %reduce-scatter.3.cloned.1.call-done = bf16[128,1280]{1,0:T(8,128)(2,1)} async-done(((bf16[2048,1280]{1,0:T(8,128)(2,1)}), bf16[128,1280]{1,0:T(8,128)(2,1)}) %reduce-scatter.3.cloned.1.call-update) | async-done | bytes 327696 | tf_op jit(solution)/shard_map/reduce_scatter | solution.py:213
  234.7 1.1 fusion.14
  235.9 1.3 multiply_reduce_fusion.1
  237.2 2.1 multiply_convert_fusion.1
  239.4 41.9 %all-gather.8.cloned.1.call-done = bf16[2048,1280]{1,0:T(8,128)(2,1)} async-done(((bf16[128,1280]{1,0:T(8,128)(2,1)}), bf16[2048,1280]{1,0:T(8,128)(2,1)}) %all-gather.8.cloned.1.call-update) | async-done | bytes 5242896 | tf_op jit(solution)/shard_map/all_gather | solution.py:222
  281.2 5.9 %convolution_multiply_fusion = f32[2048,320]{0,1:T(8,128)} fusion(bf16[2048,1280]{1,0:T(8,128)(2,1)} %all-gather.8.cloned.1.call-done, bf16[1280,320]{0,1:T(8,128)(2,1)S(1)} %copy-done.12, f32[320]{0:T(512)S(1)} %copy-done.14), kind=kOutput, calls=%fused_computation.17 | convolution fusion | flops 1678376960 | bytes 8684800 | tf_op jit(solution)/shard_map/dot_general | solution.py:117
  287.2 8.7 %convolution_convert_fusion.1 = bf16[2048,1280]{1,0:T(8,128)(2,1)} fusion(bf16[320,1280]{1,0:T(8,128)(2,1)S(1)} %copy-done, bf16[2048,1280]{1,0:T(8,128)(2,1)} %all-gather.8.cloned.1.call-done, bf16[1280,320]{0,1:T(8,128)(2,1)S(1)} %copy-done.13, f32[2048,320]{0,1:T(8,128)} %convolution_multiply_fusion, f32[320]{0:T(512)S(1)} %copy-done.15), kind=kOutput, calls=%fused_computation.14 | convolution fusion | flops 3362652160 | bytes 14746880 | tf_op jit(solution)/shard_map/dot_general | solution.py:229
  295.9 63.5 %reduce-scatter.5.cloned.1.call-done = bf16[128,1280]{1,0:T(8,128)(2,1)} async-done(((bf16[2048,1280]{1,0:T(8,128)(2,1)}), bf16[128,1280]{1,0:T(8,128)(2,1)}) %reduce-scatter.5.cloned.1.call-update) | async-done | bytes 327696 | tf_op jit(solution)/shard_map/reduce_scatter | solution.py:228
  359.4 1.1 fusion.16
  360.6 1.3 multiply_reduce_fusion
  361.9 2.1 multiply_convert_fusion
  (136 shorter events, 25.1 us)
Async XLA Ops:
  6.5 280.7 %copy-start = (bf16[320,1280]{1,0:T(8,128)(2,1)S(1)}, bf16[320,1280]{1,0:T(8,128)(2,1)}, u32[]{:S(2)}) copy-start(bf16[320,1280]{1,0:T(8,128)(2,1)} %param.36) | copy-start | bytes 2457604
  6.5 42.0 %copy-start.2 = (bf16[128,1280]{1,0:T(8,128)(2,1)S(1)}, bf16[128,1280]{1,0:T(8,128)(2,1)}, u32[]{:S(2)}) copy-start(bf16[128,1280]{1,0:T(8,128)(2,1)} %param.20) | copy-start | bytes 983044
  6.5 86.1 %all-gather.6.cloned.1.call-start = ((), (), s32[]{:S(2)}) async-start(), calls=%async_computation.3 | async-start | bytes 1114112 | tf_op jit(solution)/shard_map/all_gather | solution.py:156
  10.5 103.5 %all-gather.4.cloned.1.call-start = ((), (), s32[]{:S(2)}) async-start(), calls=%async_computation.2 | async-start | bytes 2785280 | tf_op jit(solution)/shard_map/all_gather | solution.py:158
  10.5 38.7 %collective-permute-start = (bf16[128,1280]{1,0:T(8,128)(2,1)}, bf16[128,1280]{1,0:T(8,128)(2,1)S(1)}, u32[]{:S(2)}, u32[]{:S(2)}) collective-permute-start(bf16[128,1280]{1,0:T(8,128)(2,1)} %param.20), channel_id=1, source_target_pairs={{0,1},{1,2},{2,3},{3,4},{4,5},{5,6},{6,7},{7,8},{8,9},{9,10},{10,1... | collective-permute-start | bytes 983048 | tf_op jit(solution)/shard_map/ppermute | solution.py:35
  10.6 38.7 %collective-permute-start.1 = (bf16[128,1280]{1,0:T(8,128)(2,1)}, bf16[128,1280]{1,0:T(8,128)(2,1)S(1)}, u32[]{:S(2)}, u32[]{:S(2)}) collective-permute-start(bf16[128,1280]{1,0:T(8,128)(2,1)} %param.20), channel_id=1, source_target_pairs={{0,15},{1,0},{2,1},{3,2},{4,3},{5,4},{6,5},{7,6},{8,7},{9,8},{10,9... | collective-permute-start | bytes 983048 | tf_op jit(solution)/shard_map/ppermute | solution.py:40
  15.9 218.8 %reduce-scatter.3.cloned.1.call-start = ((), (), s32[]{:S(2)}) async-start(), calls=%async_computation.4 | async-start | bytes 5570560 | tf_op jit(solution)/shard_map/reduce_scatter | solution.py:213
  49.3 7.7 %collective-permute-start.2 = (bf16[128,1280]{1,0:T(8,128)(2,1)S(1)}, bf16[128,1280]{1,0:T(8,128)(2,1)S(1)}, u32[]{:S(2)}, u32[]{:S(2)}) collective-permute-start(bf16[128,1280]{1,0:T(8,128)(2,1)S(1)} %collective-permute-done), channel_id=1, source_target_pairs={{0,1},{1,2},{2,3},{3,4},{4,5},{5,6},{6,7},{7,8},{8,9},{9,10},{10,1... | collective-permute-start | bytes 983048 | tf_op jit(solution)/shard_map/ppermute | solution.py:35
  49.3 7.7 %collective-permute-start.3 = (bf16[128,1280]{1,0:T(8,128)(2,1)S(1)}, bf16[128,1280]{1,0:T(8,128)(2,1)S(1)}, u32[]{:S(2)}, u32[]{:S(2)}) collective-permute-start(bf16[128,1280]{1,0:T(8,128)(2,1)S(1)} %collective-permute-done.1), channel_id=1, source_target_pairs={{0,15},{1,0},{2,1},{3,2},{4,3},{5,4},{6,5},{7,6},{8,7},{9,8},{10,9... | collective-permute-start | bytes 983048 | tf_op jit(solution)/shard_map/ppermute | solution.py:40
  57.0 7.7 %collective-permute-start.4 = (bf16[128,1280]{1,0:T(8,128)(2,1)S(1)}, bf16[128,1280]{1,0:T(8,128)(2,1)S(1)}, u32[]{:S(2)}, u32[]{:S(2)}) collective-permute-start(bf16[128,1280]{1,0:T(8,128)(2,1)S(1)} %collective-permute-done.2), channel_id=1, source_target_pairs={{0,1},{1,2},{2,3},{3,4},{4,5},{5,6},{6,7},{7,8},{8,9},{9,10},{10,1... | collective-permute-start | bytes 983048 | tf_op jit(solution)/shard_map/ppermute | solution.py:35
  57.0 7.7 %collective-permute-start.5 = (bf16[128,1280]{1,0:T(8,128)(2,1)S(1)}, bf16[128,1280]{1,0:T(8,128)(2,1)S(1)}, u32[]{:S(2)}, u32[]{:S(2)}) collective-permute-start(bf16[128,1280]{1,0:T(8,128)(2,1)S(1)} %collective-permute-done.3), channel_id=1, source_target_pairs={{0,15},{1,0},{2,1},{3,2},{4,3},{5,4},{6,5},{7,6},{8,7},{9,8},{10,9... | collective-permute-start | bytes 983048 | tf_op jit(solution)/shard_map/ppermute | solution.py:40
  64.7 7.7 %collective-permute-start.6 = (bf16[128,1280]{1,0:T(8,128)(2,1)S(1)}, bf16[128,1280]{1,0:T(8,128)(2,1)S(1)}, u32[]{:S(2)}, u32[]{:S(2)}) collective-permute-start(bf16[128,1280]{1,0:T(8,128)(2,1)S(1)} %collective-permute-done.4), channel_id=1, source_target_pairs={{0,1},{1,2},{2,3},{3,4},{4,5},{5,6},{6,7},{7,8},{8,9},{9,10},{10,1... | collective-permute-start | bytes 983048 | tf_op jit(solution)/shard_map/ppermute | solution.py:35
  64.7 7.7 %collective-permute-start.7 = (bf16[128,1280]{1,0:T(8,128)(2,1)S(1)}, bf16[128,1280]{1,0:T(8,128)(2,1)S(1)}, u32[]{:S(2)}, u32[]{:S(2)}) collective-permute-start(bf16[128,1280]{1,0:T(8,128)(2,1)S(1)} %collective-permute-done.5), channel_id=1, source_target_pairs={{0,15},{1,0},{2,1},{3,2},{4,3},{5,4},{6,5},{7,6},{8,7},{9,8},{10,9... | collective-permute-start | bytes 983048 | tf_op jit(solution)/shard_map/ppermute | solution.py:40
  72.4 7.7 %collective-permute-start.8 = (bf16[128,1280]{1,0:T(8,128)(2,1)S(1)}, bf16[128,1280]{1,0:T(8,128)(2,1)S(1)}, u32[]{:S(2)}, u32[]{:S(2)}) collective-permute-start(bf16[128,1280]{1,0:T(8,128)(2,1)S(1)} %collective-permute-done.6), channel_id=1, source_target_pairs={{0,1},{1,2},{2,3},{3,4},{4,5},{5,6},{6,7},{7,8},{8,9},{9,10},{10,1... | collective-permute-start | bytes 983048 | tf_op jit(solution)/shard_map/ppermute | solution.py:35
  72.4 7.7 %collective-permute-start.9 = (bf16[128,1280]{1,0:T(8,128)(2,1)S(1)}, bf16[128,1280]{1,0:T(8,128)(2,1)S(1)}, u32[]{:S(2)}, u32[]{:S(2)}) collective-permute-start(bf16[128,1280]{1,0:T(8,128)(2,1)S(1)} %collective-permute-done.7), channel_id=1, source_target_pairs={{0,15},{1,0},{2,1},{3,2},{4,3},{5,4},{6,5},{7,6},{8,7},{9,8},{10,9... | collective-permute-start | bytes 983048 | tf_op jit(solution)/shard_map/ppermute | solution.py:40
  80.1 7.7 %collective-permute-start.10 = (bf16[128,1280]{1,0:T(8,128)(2,1)S(1)}, bf16[128,1280]{1,0:T(8,128)(2,1)S(1)}, u32[]{:S(2)}, u32[]{:S(2)}) collective-permute-start(bf16[128,1280]{1,0:T(8,128)(2,1)S(1)} %collective-permute-done.8), channel_id=1, source_target_pairs={{0,1},{1,2},{2,3},{3,4},{4,5},{5,6},{6,7},{7,8},{8,9},{9,10},{10,1... | collective-permute-start | bytes 983048 | tf_op jit(solution)/shard_map/ppermute | solution.py:35
  80.1 7.9 %collective-permute-start.11 = (bf16[128,1280]{1,0:T(8,128)(2,1)S(1)}, bf16[128,1280]{1,0:T(8,128)(2,1)S(1)}, u32[]{:S(2)}, u32[]{:S(2)}) collective-permute-start(bf16[128,1280]{1,0:T(8,128)(2,1)S(1)} %collective-permute-done.9), channel_id=1, source_target_pairs={{0,15},{1,0},{2,1},{3,2},{4,3},{5,4},{6,5},{7,6},{8,7},{9,8},{10,9... | collective-permute-start | bytes 983048 | tf_op jit(solution)/shard_map/ppermute | solution.py:40
  87.8 8.9 %collective-permute-start.12 = (bf16[128,1280]{1,0:T(8,128)(2,1)S(1)}, bf16[128,1280]{1,0:T(8,128)(2,1)S(1)}, u32[]{:S(2)}, u32[]{:S(2)}) collective-permute-start(bf16[128,1280]{1,0:T(8,128)(2,1)S(1)} %collective-permute-done.10), channel_id=1, source_target_pairs={{0,1},{1,2},{2,3},{3,4},{4,5},{5,6},{6,7},{7,8},{8,9},{9,10},{10,1... | collective-permute-start | bytes 983048 | tf_op jit(solution)/shard_map/ppermute | solution.py:35
  88.1 9.5 %collective-permute-start.13 = (bf16[128,1280]{1,0:T(8,128)(2,1)S(1)}, bf16[128,1280]{1,0:T(8,128)(2,1)}, u32[]{:S(2)}, u32[]{:S(2)}) collective-permute-start(bf16[128,1280]{1,0:T(8,128)(2,1)S(1)} %collective-permute-done.11), channel_id=1, source_target_pairs={{0,15},{1,0},{2,1},{3,2},{4,3},{5,4},{6,5},{7,6},{8,7},{9,8},{10,9... | collective-permute-start | bytes 983048 | tf_op jit(solution)/shard_map/ppermute | solution.py:40
  95.9 27.8 %copy-start.11 = (s32[1,8]{1,0:T(1,128)S(1)}, s32[1,8]{1,0:T(1,128)}, u32[]{:S(2)}) copy-start(s32[1,8]{1,0:T(1,128)} %param.23) | copy-start | bytes 100
  96.8 7.7 %collective-permute-start.14 = (bf16[128,1280]{1,0:T(8,128)(2,1)S(1)}, bf16[128,1280]{1,0:T(8,128)(2,1)S(1)}, u32[]{:S(2)}, u32[]{:S(2)}) collective-permute-start(bf16[128,1280]{1,0:T(8,128)(2,1)S(1)} %collective-permute-done.12), channel_id=1, source_target_pairs={{0,1},{1,2},{2,3},{3,4},{4,5},{5,6},{6,7},{7,8},{8,9},{9,10},{10,1... | collective-permute-start | bytes 983048 | tf_op jit(solution)/shard_map/ppermute | solution.py:35
  133.0 4.1 %copy-start.5 = (bf16[1280,192]{0,1:T(8,128)(2,1)S(1)}, bf16[1280,192]{0,1:T(8,128)(2,1)}, u32[]{:S(2)}) copy-start(bf16[1280,192]{0,1:T(8,128)(2,1)} %param.26) | copy-start | bytes 1474564
  137.1 4.5 %copy-start.4 = (bf16[2048,1,2,64]{0,3,2,1:T(8,128)(2,1)S(1)}, bf16[2048,1,2,64]{0,3,2,1:T(8,128)(2,1)}, u32[]{:S(2)}) copy-start(bf16[2048,1,2,64]{0,3,2,1:T(8,128)(2,1)} %broadcast_select_fusion) | copy-start | bytes 1572868
  141.5 1.6 copy-start.10
  141.5 1.9 copy-start.6
  141.5 1.9 copy-start.16
  143.4 22.7 %copy-start.7 = (bf16[64,1280]{1,0:T(8,128)(2,1)S(1)}, bf16[64,1280]{1,0:T(8,128)(2,1)}, u32[]{:S(2)}) copy-start(bf16[64,1280]{1,0:T(8,128)(2,1)} %param.30) | copy-start | bytes 491524
  169.9 65.9 %copy-start.3 = (bf16[128,1280]{1,0:T(8,128)(2,1)S(1)}, bf16[128,1280]{1,0:T(8,128)(2,1)}, u32[]{:S(2)}) copy-start(bf16[128,1280]{1,0:T(8,128)(2,1)} %param.20) | copy-start | bytes 983044
  169.9 65.9 %copy-start.8 = (f32[1280]{0:T(1024)S(1)}, f32[1280]{0:T(1024)}, u32[]{:S(2)}) copy-start(f32[1280]{0:T(1024)} %param.31) | copy-start | bytes 15364
  169.9 111.3 %copy-start.12 = (bf16[1280,320]{0,1:T(8,128)(2,1)S(1)}, bf16[1280,320]{0,1:T(8,128)(2,1)}, u32[]{:S(2)}) copy-start(bf16[1280,320]{0,1:T(8,128)(2,1)} %param.33) | copy-start | bytes 2457604
  169.9 111.3 %copy-start.14 = (f32[320]{0:T(512)S(1)}, f32[320]{0:T(512)}, u32[]{:S(2)}) copy-start(f32[320]{0:T(512)} %param.35) | copy-start | bytes 3844
  170.0 111.3 %all-gather.8.cloned.1.call-start = ((), (), s32[]{:S(2)}) async-start(), calls=%async_computation.5 | async-start | bytes 5570560 | tf_op jit(solution)/shard_map/all_gather | solution.py:222
  239.3 47.9 %copy-start.13 = (bf16[1280,320]{0,1:T(8,128)(2,1)S(1)}, bf16[1280,320]{0,1:T(8,128)(2,1)}, u32[]{:S(2)}) copy-start(bf16[1280,320]{0,1:T(8,128)(2,1)} %param.32) | copy-start | bytes 2457604
  239.3 47.9 %copy-start.15 = (f32[320]{0:T(512)S(1)}, f32[320]{0:T(512)}, u32[]{:S(2)}) copy-start(f32[320]{0:T(512)} %param.34) | copy-start | bytes 3844
  239.3 120.1 %reduce-scatter.5.cloned.1.call-start = ((), (), s32[]{:S(2)}) async-start(), calls=%async_computation.6 | async-start | bytes 5570560 | tf_op jit(solution)/shard_map/reduce_scatter | solution.py:228
  295.9 64.6 %copy-start.1 = (bf16[128,1280]{1,0:T(8,128)(2,1)S(1)}, bf16[128,1280]{1,0:T(8,128)(2,1)}, u32[]{:S(2)}) copy-start(bf16[128,1280]{1,0:T(8,128)(2,1)} %multiply_convert_fusion.1) | copy-start | bytes 983044
  295.9 64.6 %copy-start.9 = (f32[1280]{0:T(1024)S(1)}, f32[1280]{0:T(1024)}, u32[]{:S(2)}) copy-start(f32[1280]{0:T(1024)} %param.37) | copy-start | bytes 15364
Sparse Core Ops, SparseCore 0:
  10.6 50.1 all-gather.5
  63.3 50.6 all-gather.3
  170.1 64.5 reduce-scatter.2
  239.4 41.7 all-gather.7
  296.1 63.3 reduce-scatter.4
